TPU v7x, 128 devices: a whole 4x4x4 slice. The times are simulated.
128 devices in a mesh: sx: 8 (over y, core), sy: 16 (over z, x).
Axes of the slice: x: 4, y: 4, z: 4, core: 2. Of those that a mesh axis runs over, the one named last changes fastest.
Arguments:
- features: bfloat16 [131072, 384], P(('sx', 'sy'))
- cotangent: bfloat16 [131072, 384], P(('sx', 'sy')), may hold values from -6 to 6
- hilbert_rank: int32 [131072], P(('sx', 'sy')), may hold values from 0 to 131071, as said below
- w_qkv: bfloat16 [384, 1152], replicated
- w_proj: bfloat16 [384, 384], replicated, may hold values from -0.3125 to 0.3125
Outputs:
- outputs: bfloat16 [131072, 384], P(('sx', 'sy'))
- grad_features: bfloat16 [131072, 384], P(('sx', 'sy'))
- grad_qkv: float32 [384, 1152], replicated
- grad_proj: float32 [384, 384], replicated
Inputs may be any that keep to these rules, and one draw needn't show every extreme that they name: hilbert_rank is a permutation. Hilbert positions t * 1024 to (t + 1) * 1024 - 1 belong to device t. Every device sends rows to every device, 4 to 16 rows to each, and every device has 16 rows for some owners and receives 16 rows from some devices.
All inputs are finite; a program needn't handle non-finite values.
Results may differ from a plain program's by a relative error of at most 0.004.
The roundings to bfloat16 on the way count: a program that leaves them out, or rounds other values in their place, can miss the bound.
Values may be sent and summed in bfloat16 or wider, within the bound.
A program may use at most 64 MiB of HBM per device.

v0:
```python
import math
import jax
import jax.numpy as jnp
from jax import lax
from jax.sharding import PartitionSpec as P

HEADS = 24
PATCH = 1024


def contract(left_op, right_op, left_dim, right_dim):
    return lax.dot_general(
        left_op,
        right_op,
        (((left_dim,), (right_dim,)), ((), ())),
        preferred_element_type=jnp.float32,
    )


def head_pass(query_rows, key_rows, value_rows, grad_slice):
    score_scale = query_rows.shape[1] ** (-0.5)
    scores = contract(query_rows, key_rows, 1, 1) * score_scale
    shifted = jnp.exp(scores - jnp.max(scores, axis=1, keepdims=True))
    prob_full = shifted / jnp.sum(shifted, axis=1, keepdims=True)
    prob_low = prob_full.astype(jnp.bfloat16)
    attended = jnp.dot(prob_low, value_rows, preferred_element_type=jnp.float32).astype(
        jnp.bfloat16
    )
    dprobs = contract(grad_slice, value_rows, 1, 1)
    dscores = (
        prob_full * (dprobs - jnp.sum(dprobs * prob_full, axis=1, keepdims=True)) * score_scale
    ).astype(jnp.bfloat16)
    dquery = jnp.dot(dscores, key_rows, preferred_element_type=jnp.float32).astype(jnp.bfloat16)
    dkey_rows = contract(dscores, query_rows, 0, 0).astype(jnp.bfloat16)
    dvalue = contract(prob_low, grad_slice, 0, 0).astype(jnp.bfloat16)
    return (attended, dquery, dkey_rows, dvalue)


def patch_pass(block_rows, block_grads, w_qkv, w_proj, head_count):
    feat_width = block_rows.shape[1]
    head_dim = feat_width // head_count
    values = block_rows.astype(jnp.float32)
    row_mean = jnp.mean(values, axis=1, keepdims=True)
    centred = values - row_mean
    inv_std = lax.rsqrt(jnp.mean(centred * centred, axis=1, keepdims=True) + 1e-05)
    normed = centred * inv_std
    normed_low = normed.astype(jnp.bfloat16)
    projected = jnp.dot(normed_low, w_qkv, preferred_element_type=jnp.float32).astype(jnp.bfloat16)
    upstream = contract(block_grads, w_proj, 1, 1).astype(jnp.bfloat16)

    def one_head(head_index):
        head_start = head_index * head_dim
        query_rows = lax.dynamic_slice_in_dim(projected, head_start, head_dim, 1)
        key_rows = lax.dynamic_slice_in_dim(projected, head_start + feat_width, head_dim, 1)
        value_rows = lax.dynamic_slice_in_dim(projected, head_start + 2 * feat_width, head_dim, 1)
        grad_slice = lax.dynamic_slice_in_dim(upstream, head_start, head_dim, 1)
        return head_pass(query_rows, key_rows, value_rows, grad_slice)

    heads_out = lax.map(one_head, jnp.arange(head_count, dtype=jnp.int32))

    def merge_heads(stacked):
        return jnp.transpose(stacked, (1, 0, 2)).reshape(stacked.shape[1], feat_width)

    attended = merge_heads(heads_out[0])
    dprojected = jnp.concatenate(
        [merge_heads(heads_out[1]), merge_heads(heads_out[2]), merge_heads(heads_out[3])], axis=1
    )
    mixed_out = jnp.dot(attended, w_proj, preferred_element_type=jnp.float32)
    output = (values + mixed_out).astype(jnp.bfloat16)
    dnormed = contract(dprojected, w_qkv, 1, 1)
    dnorm_mean = jnp.mean(dnormed, axis=1, keepdims=True)
    cross_mean = jnp.mean(dnormed * normed, axis=1, keepdims=True)
    dinput = inv_std * (dnormed - dnorm_mean - normed * cross_mean)
    grad_input = (block_grads.astype(jnp.float32) + dinput).astype(jnp.bfloat16)
    return (output, grad_input, normed_low, dprojected, attended)


def on_device(features, cotangent, hilbert_rank, w_qkv, w_proj):
    row_count = features.shape[0]
    feat_width = features.shape[1]
    size_x = lax.axis_size("sx")
    size_y = lax.axis_size("sy")
    devices = size_x * size_y
    capacity = 2 * row_count // devices
    slot_total = devices * capacity
    owner_dev = hilbert_rank // row_count
    place_row = hilbert_rank % row_count
    sort_order = jnp.argsort(hilbert_rank)
    owner_sorted = owner_dev[sort_order]
    labels = jnp.arange(devices, dtype=jnp.int32)
    counts = jnp.sum((owner_dev[:, None] == labels[None, :]).astype(jnp.int32), axis=0)
    starts = jnp.cumsum(counts) - counts
    first_slot = jnp.sum(
        jnp.where(owner_sorted[:, None] == labels[None, :], starts[None, :], 0), axis=1
    )
    slot_sorted = owner_sorted * capacity + jnp.arange(row_count, dtype=jnp.int32) - first_slot
    slot_index = jnp.zeros((row_count,), jnp.int32).at[sort_order].set(slot_sorted)
    send_rows = jnp.zeros((slot_total, feat_width), features.dtype).at[slot_index].set(features)
    send_grads = jnp.zeros((slot_total, feat_width), cotangent.dtype).at[slot_index].set(cotangent)
    send_place = jnp.full((slot_total,), row_count, jnp.int32).at[slot_index].set(place_row)
    got_rows, got_grads, got_place = (
        lax.all_to_all(send_rows, ("sx", "sy"), split_axis=0, concat_axis=0, tiled=True),
        lax.all_to_all(send_grads, ("sx", "sy"), split_axis=0, concat_axis=0, tiled=True),
        lax.all_to_all(send_place, ("sx", "sy"), split_axis=0, concat_axis=0, tiled=True),
    )
    curve_rows = (
        jnp.zeros((row_count, feat_width), jnp.bfloat16).at[got_place].set(got_rows, mode="drop")
    )
    curve_grads = (
        jnp.zeros((row_count, feat_width), jnp.bfloat16).at[got_place].set(got_grads, mode="drop")
    )
    patch_total = row_count // PATCH

    def run_patch(both_blocks):
        return patch_pass(both_blocks[0], both_blocks[1], w_qkv, w_proj, HEADS)

    results = lax.map(
        run_patch,
        (
            curve_rows.reshape(patch_total, PATCH, feat_width),
            curve_grads.reshape(patch_total, PATCH, feat_width),
        ),
    )
    curve_out = results[0].reshape(row_count, feat_width)
    curve_grad = results[1].reshape(row_count, feat_width)
    normed_low = results[2].reshape(row_count, feat_width)
    dprojected = results[3].reshape(row_count, 3 * feat_width)
    attended = results[4].reshape(row_count, feat_width)
    grad_terms = (contract(normed_low, dprojected, 0, 0), contract(attended, curve_grads, 0, 0))
    back_place = jnp.minimum(got_place, row_count - 1)
    back_rows = curve_out[back_place]
    back_grads = curve_grad[back_place]
    ret_rows, ret_grads = (
        lax.all_to_all(back_rows, ("sx", "sy"), split_axis=0, concat_axis=0, tiled=True),
        lax.all_to_all(back_grads, ("sx", "sy"), split_axis=0, concat_axis=0, tiled=True),
    )
    grad_sums = lax.psum((grad_terms[0], grad_terms[1]), ("sx", "sy"))
    grad_scale = 1.0 / math.sqrt(row_count * devices)
    return (
        ret_rows[slot_index],
        ret_grads[slot_index],
        grad_sums[0] * grad_scale,
        grad_sums[1] * grad_scale,
    )


def solution(mesh):
    in_specs = (P(("sx", "sy"), None), P(("sx", "sy"), None), P(("sx", "sy")), P(), P())
    out_specs = (P(("sx", "sy"), None), P(("sx", "sy"), None), P(), P())
    return jax.shard_map(
        on_device, mesh=mesh, in_specs=in_specs, out_specs=out_specs, check_vma=False
    )
```

profile of v0, /device:TPU:1, one launch (start us, length us, event | category | flops | bytes accessed | tf_op | source)
XLA Modules:
  0.0 736.6 jit_solution(12952684937199685522)
XLA Ops:
  7.2 5.1 sort.17
  13.2 4.5 gather_fusion
  18.6 4.3 scatter_custom_fusion
  22.9 4.3 scatter_custom_fusion.1
  27.9 11.5 %all-to-all-start = ((s32[128,16,1]{1,2,0:T(1,128)}), s32[128,16,1]{1,2,0:T(1,128)S(1)}, u32[]{:S(2)}, u32[]{:S(2)}) async-start(s32[128,16,1]{1,2,0:T(1,128)} %bitcast.6), calls=%async_computation | async-start | bytes 131072 | tf_op jit(solution)/shard_map/all_to_all | solution.py:104
  39.4 6.8 scatter_custom_fusion.2
  49.8 6.8 all-to-all-start.1
  56.6 6.8 scatter_custom_fusion.4
  63.4 17.3 %all-to-all-done.1 = bf16[128,16,384]{2,1,0:T(8,128)(2,1)S(1)} async-done(((bf16[128,16,384]{2,1,0:T(8,128)(2,1)}), bf16[128,16,384]{2,1,0:T(8,128)(2,1)S(1)}, u32[]{:S(2)}, u32[]{:S(2)}) %all-to-all-start.1) | async-done | bytes 1572896 | tf_op jit(solution)/shard_map/all_to_all | solution.py:102
  81.8 4.9 all-to-all-start.2
  89.6 9.9 %scatter_custom_fusion.3 = bf16[1024,384]{1,0:T(8,128)(2,1)S(1)} fusion(s32[2048]{0:T(1024)} %bitcast.80, bf16[2048,384]{1,0:T(8,128)(2,1)} %bitcast.76, bf16[]{:T(256)} %constant.129.clone.1), kind=kCustom, calls=%fused_computation.78 | custom fusion | bytes 786944 | tf_op jit(solution)/shard_map/scatter | solution.py:107
  100.9 10.0 %all-to-all-done.2 = bf16[128,16,384]{2,1,0:T(8,128)(2,1)S(1)} async-done(((bf16[128,16,384]{2,1,0:T(8,128)(2,1)}), bf16[128,16,384]{2,1,0:T(8,128)(2,1)S(1)}, u32[]{:S(2)}, u32[]{:S(2)}) %all-to-all-start.2) | async-done | bytes 1572896 | tf_op jit(solution)/shard_map/all_to_all | solution.py:103
  112.1 9.9 %scatter_custom_fusion.5 = bf16[1024,384]{1,0:T(8,128)(2,1)S(1)} fusion(s32[2048]{0:T(1024)} %bitcast.81, bf16[2048,384]{1,0:T(8,128)(2,1)} %bitcast.75, bf16[]{:T(256)} %constant.129.clone.1), kind=kCustom, calls=%fused_computation.76 | custom fusion | bytes 786944 | tf_op jit(solution)/shard_map/scatter | solution.py:110
  122.7 3.7 convolution_convert_fusion.4
  126.9 391.0 %while.32 = (s32[]{:T(128)}, bf16[24,1024,16]{1,2,0:T(8,128)(2,1)}, bf16[24,1024,16]{1,2,0:T(8,128)(2,1)}, bf16[24,1024,16]{1,2,0:T(8,128)(2,1)}, bf16[24,1024,1...) while((s32[]{:T(128)}, bf16[24,1024,16]{1,2,0:T(8,128)(2,1)}, ...), condition=%wide.region_16.17_spmd, body=%wide.region_12.16_spmd.sunk | while | flops 227603472 | bytes 42127728 | solution.py:59
  519.7 9.0 %gather_fusion.1 = bf16[2048,384]{1,0:T(8,128)(2,1)} fusion(bf16[1024,384]{1,0:T(8,128)(2,1)S(1)} %fusion.41, s32[2048]{0:T(1024)S(1)} %broadcast_clamp_fusion), kind=kCustom, calls=%fused_computation.1 | custom fusion | bytes 3153920 | tf_op jit(solution)/shard_map/gather | solution.py:131
  528.8 5.0 all-to-all-start.3
  534.1 3.7 fusion.62
  543.8 3.9 fusion.42
  551.8 9.0 %gather_fusion.3 = bf16[2048,384]{1,0:T(8,128)(2,1)} fusion(bf16[1024,384]{1,0:T(8,128)(2,1)S(1)} %fusion.39, s32[2048]{0:T(1024)S(1)} %broadcast_clamp_fusion), kind=kCustom, calls=%fused_computation.3 | custom fusion | bytes 3153920 | tf_op jit(solution)/shard_map/gather | solution.py:132
  560.8 10.3 %all-to-all-start.4 = ((bf16[128,16,384]{2,1,0:T(8,128)(2,1)}), bf16[128,16,384]{2,1,0:T(8,128)(2,1)}, u32[]{:S(2)}, u32[]{:S(2)}) async-start(bf16[128,16,384]{2,1,0:T(8,128)(2,1)} %bitcast.74), calls=%async_computation.4 | async-start | bytes 3145728 | tf_op jit(solution)/shard_map/all_to_all | solution.py:135
  571.1 142.4 %all-reduce.3.cloned.1.call-done = (f32[384,1152]{1,0:T(8,128)}, f32[384,384]{1,0:T(8,128)}) async-done(((f32[384,1152]{1,0:T(8,128)}, f32[384,384]{1,0:T(8,128)}), (f32[384,1152]{1,0:T(8,128)}, f32[384,384]{1,0:T(8,128)})) %all-reduce.3.cloned.1.call-update) | async-done | bytes 2359312 | tf_op jit(solution)/shard_map/psum | solution.py:137
  718.3 5.0 gather_fusion.2
  723.3 6.5 gather_fusion.4
  (284 shorter events, 404.8 us)
Async XLA Ops:
  7.2 115.5 %copy-start = (bf16[384,1152]{1,0:T(8,128)(2,1)S(1)}, bf16[384,1152]{1,0:T(8,128)(2,1)}, u32[]{:S(2)}) copy-start(bf16[384,1152]{1,0:T(8,128)(2,1)} %param.10) | copy-start | bytes 2654212
  27.9 21.2 %all-to-all-start = ((s32[128,16,1]{1,2,0:T(1,128)}), s32[128,16,1]{1,2,0:T(1,128)S(1)}, u32[]{:S(2)}, u32[]{:S(2)}) async-start(s32[128,16,1]{1,2,0:T(1,128)} %bitcast.6), calls=%async_computation | async-start | bytes 131072 | tf_op jit(solution)/shard_map/all_to_all | solution.py:104
  49.1 0.6 copy-start.9
  49.8 30.9 %all-to-all-start.1 = ((bf16[128,16,384]{2,1,0:T(8,128)(2,1)}), bf16[128,16,384]{2,1,0:T(8,128)(2,1)S(1)}, u32[]{:S(2)}, u32[]{:S(2)}) async-start(bf16[128,16,384]{2,1,0:T(8,128)(2,1)} %bitcast.8), calls=%async_computation.1 | async-start | bytes 3145728 | tf_op jit(solution)/shard_map/all_to_all | solution.py:102
  80.7 1.1 copy-start.7
  81.8 29.1 %all-to-all-start.2 = ((bf16[128,16,384]{2,1,0:T(8,128)(2,1)}), bf16[128,16,384]{2,1,0:T(8,128)(2,1)S(1)}, u32[]{:S(2)}, u32[]{:S(2)}) async-start(bf16[128,16,384]{2,1,0:T(8,128)(2,1)} %bitcast.10), calls=%async_computation.2 | async-start | bytes 3145728 | tf_op jit(solution)/shard_map/all_to_all | solution.py:103
  86.7 35.3 %copy-start.8 = (bf16[384,384]{1,0:T(8,128)(2,1)S(1)}, bf16[384,384]{1,0:T(8,128)(2,1)}, u32[]{:S(2)}) copy-start(bf16[384,384]{1,0:T(8,128)(2,1)} %param.11) | copy-start | bytes 884740
  99.6 418.3 %copy-start.1 = (bf16[1024,384]{1,0:T(8,128)(2,1)}, bf16[1024,384]{1,0:T(8,128)(2,1)S(1)}, u32[]{:S(2)}) copy-start(bf16[1024,384]{1,0:T(8,128)(2,1)S(1)} %scatter_custom_fusion.3) | copy-start | bytes 2359300
  110.9 1.1 copy-start.6
  122.0 4.3 copy-start.5
  528.8 5.3 copy-start.11
  528.8 32.0 %all-to-all-start.3 = ((bf16[128,16,384]{2,1,0:T(8,128)(2,1)}), bf16[128,16,384]{2,1,0:T(8,128)(2,1)S(1)}, u32[]{:S(2)}, u32[]{:S(2)}) async-start(bf16[128,16,384]{2,1,0:T(8,128)(2,1)} %bitcast.73), calls=%async_computation.3 | async-start | bytes 3145728 | tf_op jit(solution)/shard_map/all_to_all | solution.py:134
  533.8 179.7 %all-reduce.3.cloned.1.call-start = ((), (), s32[]{:S(2)}) async-start(), calls=%async_computation.5 | async-start | bytes 4718592 | tf_op jit(solution)/shard_map/psum | solution.py:137
  537.8 6.0 copy-start.2
  537.8 6.0 copy-start.10
  540.9 2.9 copy-start.12
  540.9 2.9 copy-start.13
  547.8 2.1 copy-start.3
  547.8 2.1 copy-start.4
  560.8 162.5 %all-to-all-start.4 = ((bf16[128,16,384]{2,1,0:T(8,128)(2,1)}), bf16[128,16,384]{2,1,0:T(8,128)(2,1)}, u32[]{:S(2)}, u32[]{:S(2)}) async-start(bf16[128,16,384]{2,1,0:T(8,128)(2,1)} %bitcast.74), calls=%async_computation.4 | async-start | bytes 3145728 | tf_op jit(solution)/shard_map/all_to_all | solution.py:135
Sparse Core Ops, SparseCore 0:
  547.9 165.5 all-reduce.2
where the time goes:
time: 741 us; the launch traced here: 737 us
  matrix products  314 us (42%)
  waiting for transfers between devices  173 us (23%)
  local copies, waits for them, and re-layouts  114 us (15%)
  other arithmetic  66.6 us (9%)
  starting transfers between devices  38.8 us (5%)
  loops' own time  16.7 us (2%)
  between operations  14.4 us (2%)
    dot_general x100, matrix products, contract(): lax.dot_general(left_op, right_op, (((left_dim,), (right_dim,)), ((), ())...  199 us
    psum x1, waiting for transfers between devices, on_device(): grad_sums = lax.psum((grad_terms[0], grad_terms[1]), ('sx', 'sy'))  142 us
    dot_general x24, matrix products, head_pass(): jnp.dot(prob_low, value_rows, preferred_element_type=jnp.float32)  59.7 us
    dot_general x24, matrix products, head_pass(): jnp.dot(dscores, key_rows, preferred_element_type=jnp.float32)  49.5 us
    convert_element_type x24, other arithmetic, head_pass(): dscores = (prob_full * (dprobs - jnp.sum(dprobs * prob_full, axis=1, keep...  30.2 us
    dynamic_slice x24, local copies, waits for them, and re-layouts, patch_pass(): heads_out = lax.map(one_head, jnp.arange(head_count, dtype=jnp.int32))  29.7 us
    scatter x2, local copies, waits for them, and re-layouts, on_device(): jnp.zeros((row_count, feat_width), jnp.bfloat16).at[got_place]  19.9 us
    reduce_sum x24, other arithmetic, head_pass(): prob_full = shifted / jnp.sum(shifted, axis=1, keepdims=True)  17.5 us
  transfers between devices with their start and end apart: 6, of which 4 were waited for; matrix products, arithmetic and copies ran while one was open for 9% of the time, Pallas kernels for 0%

commit v1 on v0

--- a/solution.py
+++ b/solution.py
@@ -134,7 +134,12 @@
         lax.all_to_all(back_rows, ("sx", "sy"), split_axis=0, concat_axis=0, tiled=True),
         lax.all_to_all(back_grads, ("sx", "sy"), split_axis=0, concat_axis=0, tiled=True),
     )
-    grad_sums = lax.psum((grad_terms[0], grad_terms[1]), ("sx", "sy"))
+
+    def pools_group(panel):
+        v1 = lax.psum(lax.psum(panel, "sy"), "sx")
+        return v1
+
+    grad_sums = pools_group((grad_terms[0], grad_terms[1]))
     grad_scale = 1.0 / math.sqrt(row_count * devices)
     return (
         ret_rows[slot_index],

time: 741 us -> 706 us (0.953)
  local copies, waits for them, and re-layouts: 114 us -> 98.8 us
  waiting for transfers between devices: 173 us -> 159 us
    psum x1 -> x2, waiting for transfers between devices: 142 us -> 124 us  [pools_group(): v1 = lax.psum(lax.psum(panel, 'sy'), 'sx')]
    dynamic_slice x24, local copies, waits for them, and re-layouts: 29.7 us -> 14 us  [patch_pass(): heads_out = lax.map(one_head, jnp.arange(head_count, dtype=jnp.int32))]
  transfers between devices with their start and end apart: 6 -> 7, of which waited for: 4 -> 6; matrix products, arithmetic and copies ran while one was open for 9% -> 10% of each run, Pallas kernels for 0% -> 0%
where the time goes in v1:
time: 706 us; the launch traced here: 700 us
  matrix products  312 us (44%)
  waiting for transfers between devices  159 us (23%)
  local copies, waits for them, and re-layouts  98.8 us (14%)
  other arithmetic  65 us (9%)
  starting transfers between devices  34.5 us (5%)
  loops' own time  16.7 us (2%)
  between operations  14.4 us (2%)
    dot_general x100, matrix products, contract(): lax.dot_general(left_op, right_op, (((left_dim,), (right_dim,)), ((), ())...  199 us
    psum x2, waiting for transfers between devices, pools_group(): v1 = lax.psum(lax.psum(panel, 'sy'), 'sx')  124 us
    dot_general x24, matrix products, head_pass(): jnp.dot(prob_low, value_rows, preferred_element_type=jnp.float32)  59.7 us
    dot_general x24, matrix products, head_pass(): jnp.dot(dscores, key_rows, preferred_element_type=jnp.float32)  49.5 us
    convert_element_type x24, other arithmetic, head_pass(): dscores = (prob_full * (dprobs - jnp.sum(dprobs * prob_full, axis=1, keep...  30.1 us
    scatter x2, local copies, waits for them, and re-layouts, on_device(): jnp.zeros((row_count, feat_width), jnp.bfloat16).at[got_place]  19.9 us
    reduce_sum x24, other arithmetic, head_pass(): prob_full = shifted / jnp.sum(shifted, axis=1, keepdims=True)  17.5 us
    all_to_all x1, waiting for transfers between devices, on_device(): lax.all_to_all(send_rows, ('sx', 'sy'), split_axis=0, concat_axis=0, tile...  17.3 us
  transfers between devices with their start and end apart: 7, of which 6 were waited for; matrix products, arithmetic and copies ran while one was open for 10% of the time, Pallas kernels for 0%

profile of v1, /device:TPU:1, one launch (start us, length us, event | category | flops | bytes accessed | tf_op | source)
XLA Modules:
  0.0 700.3 jit_solution(6472149889551264150)
XLA Ops:
  7.2 5.1 sort.17
  13.2 4.5 gather_fusion
  18.6 4.3 scatter_custom_fusion
  22.9 4.3 scatter_custom_fusion.1
  27.9 11.5 %all-to-all-start = ((s32[128,16,1]{1,2,0:T(1,128)}), s32[128,16,1]{1,2,0:T(1,128)S(1)}, u32[]{:S(2)}, u32[]{:S(2)}) async-start(s32[128,16,1]{1,2,0:T(1,128)} %bitcast.6), calls=%async_computation | async-start | bytes 131072 | tf_op jit(solution)/shard_map/all_to_all | solution.py:104
  39.4 6.8 scatter_custom_fusion.2
  49.8 6.8 all-to-all-start.1
  56.6 6.8 scatter_custom_fusion.4
  63.4 17.3 %all-to-all-done.1 = bf16[128,16,384]{2,1,0:T(8,128)(2,1)S(1)} async-done(((bf16[128,16,384]{2,1,0:T(8,128)(2,1)}), bf16[128,16,384]{2,1,0:T(8,128)(2,1)S(1)}, u32[]{:S(2)}, u32[]{:S(2)}) %all-to-all-start.1) | async-done | bytes 1572896 | tf_op jit(solution)/shard_map/all_to_all | solution.py:102
  81.8 4.9 all-to-all-start.2
  89.9 9.9 %scatter_custom_fusion.3 = bf16[1024,384]{1,0:T(8,128)(2,1)S(1)} fusion(s32[2048]{0:T(1024)} %bitcast.80, bf16[2048,384]{1,0:T(8,128)(2,1)} %bitcast.76, bf16[]{:T(256)} %constant.129.clone.1), kind=kCustom, calls=%fused_computation.78 | custom fusion | bytes 786944 | tf_op jit(solution)/shard_map/scatter | solution.py:107
  100.5 10.4 %all-to-all-done.2 = bf16[128,16,384]{2,1,0:T(8,128)(2,1)S(1)} async-done(((bf16[128,16,384]{2,1,0:T(8,128)(2,1)}), bf16[128,16,384]{2,1,0:T(8,128)(2,1)S(1)}, u32[]{:S(2)}, u32[]{:S(2)}) %all-to-all-start.2) | async-done | bytes 1572896 | tf_op jit(solution)/shard_map/all_to_all | solution.py:103
  112.1 9.9 %scatter_custom_fusion.5 = bf16[1024,384]{1,0:T(8,128)(2,1)S(1)} fusion(s32[2048]{0:T(1024)} %bitcast.81, bf16[2048,384]{1,0:T(8,128)(2,1)} %bitcast.75, bf16[]{:T(256)} %constant.129.clone.1), kind=kCustom, calls=%fused_computation.76 | custom fusion | bytes 786944 | tf_op jit(solution)/shard_map/scatter | solution.py:110
  125.7 375.3 %while.32 = (s32[]{:T(128)}, bf16[24,1024,16]{1,2,0:T(8,128)(2,1)}, bf16[24,1024,16]{1,2,0:T(8,128)(2,1)}, bf16[24,1024,16]{1,2,0:T(8,128)(2,1)}, bf16[24,1024,1...) while((s32[]{:T(128)}, bf16[24,1024,16]{1,2,0:T(8,128)(2,1)}, ...), condition=%wide.region_16.17_spmd, body=%wide.region_12.16_spmd.sunk | while | flops 227603472 | bytes 42127728 | solution.py:59
  503.7 3.9 fusion.42
  509.4 9.0 %gather_fusion.1 = bf16[2048,384]{1,0:T(8,128)(2,1)} fusion(bf16[1024,384]{1,0:T(8,128)(2,1)S(1)} %fusion.41, s32[2048]{0:T(1024)S(1)} %broadcast_clamp_fusion), kind=kCustom, calls=%fused_computation.1 | custom fusion | bytes 3153920 | tf_op jit(solution)/shard_map/gather | solution.py:131
  518.5 5.0 all-to-all-start.3
  534.4 9.0 %gather_fusion.3 = bf16[2048,384]{1,0:T(8,128)(2,1)} fusion(bf16[1024,384]{1,0:T(8,128)(2,1)S(1)} %fusion.39, s32[2048]{0:T(1024)S(1)} %broadcast_clamp_fusion), kind=kCustom, calls=%fused_computation.3 | custom fusion | bytes 3153920 | tf_op jit(solution)/shard_map/gather | solution.py:132
  543.4 4.3 all-to-all-done.3
  547.7 6.0 all-to-all-start.4
  553.8 68.0 %all-reduce.5.cloned.1.call-done = (f32[384,1152]{1,0:T(8,128)}, f32[384,384]{1,0:T(8,128)}) async-done(((f32[384,1152]{1,0:T(8,128)}, f32[384,384]{1,0:T(8,128)}), (f32[384,1152]{1,0:T(8,128)}, f32[384,384]{1,0:T(8,128)})) %all-reduce.5.cloned.1.call-update) | async-done | bytes 2359312 | tf_op jit(solution)/shard_map/psum | solution.py:139
  621.8 5.0 gather_fusion.2
  626.8 6.5 gather_fusion.4
  633.3 56.4 %all-reduce.7.cloned.1.call-done = (f32[384,1152]{1,0:T(8,128)}, f32[384,384]{1,0:T(8,128)}) async-done(((f32[384,1152]{1,0:T(8,128)}, f32[384,384]{1,0:T(8,128)}), (f32[384,1152]{1,0:T(8,128)}, f32[384,384]{1,0:T(8,128)})) %all-reduce.7.cloned.1.call-update) | async-done | bytes 2359312 | tf_op jit(solution)/shard_map/psum | solution.py:139
  (295 shorter events, 393.4 us)
Async XLA Ops:
  7.2 115.5 %copy-start = (bf16[384,1152]{1,0:T(8,128)(2,1)S(1)}, bf16[384,1152]{1,0:T(8,128)(2,1)}, u32[]{:S(2)}) copy-start(bf16[384,1152]{1,0:T(8,128)(2,1)} %param.10) | copy-start | bytes 2654212
  27.9 21.2 %all-to-all-start = ((s32[128,16,1]{1,2,0:T(1,128)}), s32[128,16,1]{1,2,0:T(1,128)S(1)}, u32[]{:S(2)}, u32[]{:S(2)}) async-start(s32[128,16,1]{1,2,0:T(1,128)} %bitcast.6), calls=%async_computation | async-start | bytes 131072 | tf_op jit(solution)/shard_map/all_to_all | solution.py:104
  49.8 30.9 %all-to-all-start.1 = ((bf16[128,16,384]{2,1,0:T(8,128)(2,1)}), bf16[128,16,384]{2,1,0:T(8,128)(2,1)S(1)}, u32[]{:S(2)}, u32[]{:S(2)}) async-start(bf16[128,16,384]{2,1,0:T(8,128)(2,1)} %bitcast.8), calls=%async_computation.1 | async-start | bytes 3145728 | tf_op jit(solution)/shard_map/all_to_all | solution.py:102
  80.7 1.1 copy-start.7
  81.8 29.1 %all-to-all-start.2 = ((bf16[128,16,384]{2,1,0:T(8,128)(2,1)}), bf16[128,16,384]{2,1,0:T(8,128)(2,1)S(1)}, u32[]{:S(2)}, u32[]{:S(2)}) async-start(bf16[128,16,384]{2,1,0:T(8,128)(2,1)} %bitcast.10), calls=%async_computation.2 | async-start | bytes 3145728 | tf_op jit(solution)/shard_map/all_to_all | solution.py:103
  86.7 35.3 %copy-start.10 = (bf16[384,384]{1,0:T(8,128)(2,1)S(1)}, bf16[384,384]{1,0:T(8,128)(2,1)}, u32[]{:S(2)}) copy-start(bf16[384,384]{1,0:T(8,128)(2,1)} %param.11) | copy-start | bytes 884740
  86.7 535.1 %all-reduce.5.cloned.1.call-start = ((), (), s32[]{:S(2)}) async-start(), calls=%async_computation.5 | async-start | bytes 4718592 | tf_op jit(solution)/shard_map/psum | solution.py:139
  99.8 408.5 %copy-start.1 = (bf16[1024,384]{1,0:T(8,128)(2,1)}, bf16[1024,384]{1,0:T(8,128)(2,1)S(1)}, u32[]{:S(2)}) copy-start(bf16[1024,384]{1,0:T(8,128)(2,1)S(1)} %scatter_custom_fusion.3) | copy-start | bytes 2359300
  100.5 403.1 %copy-start.12 = (f32[1024]{0:T(1024)}, f32[1024]{0:T(1024)S(1)}, u32[]{:S(2)}) copy-start(f32[1024]{0:T(1024)S(1)} %add_rsqrt_fusion) | copy-start | bytes 12292
  110.9 1.1 copy-start.6
  122.0 379.0 %copy-start.5 = (bf16[1024,384]{1,0:T(8,128)(2,1)}, bf16[1024,384]{1,0:T(8,128)(2,1)S(1)}, u32[]{:S(2)}) copy-start(bf16[1024,384]{1,0:T(8,128)(2,1)S(1)} %scatter_custom_fusion.5) | copy-start | bytes 2359300
  501.0 2.6 copy-start.15
  501.0 2.7 copy-start.17
  507.6 0.7 copy-start.14
  507.6 1.1 copy-start.8
  518.5 5.0 copy-start.16
  518.5 29.2 %all-to-all-start.3 = ((bf16[128,16,384]{2,1,0:T(8,128)(2,1)}), bf16[128,16,384]{2,1,0:T(8,128)(2,1)S(1)}, u32[]{:S(2)}, u32[]{:S(2)}) async-start(bf16[128,16,384]{2,1,0:T(8,128)(2,1)} %bitcast.74), calls=%async_computation.3 | async-start | bytes 3145728 | tf_op jit(solution)/shard_map/all_to_all | solution.py:134
  527.3 3.1 copy-start.2
  527.3 3.1 copy-start.13
  530.4 2.1 copy-start.3
  530.4 2.1 copy-start.4
  547.7 79.1 %all-to-all-start.4 = ((bf16[128,16,384]{2,1,0:T(8,128)(2,1)}), bf16[128,16,384]{2,1,0:T(8,128)(2,1)}, u32[]{:S(2)}, u32[]{:S(2)}) async-start(bf16[128,16,384]{2,1,0:T(8,128)(2,1)} %bitcast.73), calls=%async_computation.4 | async-start | bytes 3145728 | tf_op jit(solution)/shard_map/all_to_all | solution.py:135
  553.8 136.0 %all-reduce.7.cloned.1.call-start = ((), (), s32[]{:S(2)}) async-start(), calls=%async_computation.6 | async-start | bytes 4718592 | tf_op jit(solution)/shard_map/psum | solution.py:139
  689.7 2.9 copy-start.9
  (1 other events, 0.6 us)
Sparse Core Ops, SparseCore 0:
  507.7 114.0 all-reduce.4
  624.3 65.3 all-reduce.6
